TPU v7x, 32 devices: a whole 2x2x4 slice. The times are simulated.
32 devices in a mesh: date: 16 (over z, y, core), strip: 2 (over x).
Axes of the slice: x: 2, y: 2, z: 4, core: 2. Of those that a mesh axis runs over, the one named last changes fastest.
Arguments:
- acquisitions: bfloat16 [32, 2, 2, 344, 640], P('date', None, None, None, 'strip'), may hold values from -6 to 6
- shifts: int32 [2, 32, 2, 5, 10], P(None, 'date', None, None, 'strip'), may hold values from -8 to 8, as said below
- fractions: int32 [2, 32, 2, 5, 10], P(None, 'date', None, None, 'strip'), may hold values from 0 to 63
- ref_dates: int32 [2], replicated, may hold values from 0 to 31, as said below
Outputs:
- chip_corr: float32 [2, 32, 2, 5, 10], P(None, 'date', None, None, 'strip')
- coherence: float32 [2, 31, 2, 64, 32], P(None, None, None, 'date', 'strip')
Inputs may be any that keep to these rules, and one draw needn't show every extreme that they name: `shifts`: zero at every chip of date ref_dates[t] in tile t. `ref_dates`: the reference dates of consecutive tiles lie in different blocks of 2 dates.
All inputs are finite; a program needn't handle non-finite values.
Results may differ from a plain program's by a relative error of at most 0.0021.
Values may be sent and summed in bfloat16 or wider, within the bound.
A program may use at most 64 MiB of HBM per device.

v0:
```python
import jax
import jax.numpy as jnp
from jax import lax
from jax.sharding import PartitionSpec as P

TILE_COUNT = 2
CHIP_SIZE = 64
TAP_COUNT = 8
SUBSTEPS = 64
LOOK_AZ = 5
LOOK_RG = 20
MARGIN = 12
epsilon = 1e-06


def padded_2(block, sides, width):
    for axis, dim in sides:
        count = lax.axis_size(axis)
        forward = [(i, i + 1) for i in range(count - 1)]
        backward = [(target, source) for source, target in forward]
        low = lax.ppermute(
            lax.slice_in_dim(block, block.shape[dim] - width, None, axis=dim), axis, forward
        )
        high = lax.ppermute(lax.slice_in_dim(block, 0, width, axis=dim), axis, backward)
        block = jnp.concatenate([low, block, high], axis=dim)
    return block


def spread(value, axis, source):
    kept = jnp.where(lax.axis_index(axis) == source, value, 0).astype(value.dtype)
    return lax.psum(kept, axis)


def passed_along(block, axis, distance):
    devices = range(lax.axis_size(axis))
    route = [(i - distance, i) for i in devices if i - distance in devices]
    return lax.ppermute(block, axis, route)


def sinc_matrix(shift_part, fraction_part):
    window_size = CHIP_SIZE + 2 * MARGIN
    offset = fraction_part.astype(jnp.float32) / SUBSTEPS
    tap_axis = jnp.arange(TAP_COUNT).astype(jnp.float32)
    distance = tap_axis - (TAP_COUNT // 2 - 1) - offset[..., None]
    weights = jnp.sinc(distance) * (0.5 + 0.5 * jnp.cos(jnp.pi * distance / (TAP_COUNT // 2)))
    weights = weights / jnp.sum(weights, axis=-1, keepdims=True)
    out_rows = jnp.arange(CHIP_SIZE, dtype=jnp.int32)[:, None]
    in_rows = jnp.arange(window_size, dtype=jnp.int32)[None, :]
    matrix = jnp.zeros(shift_part.shape + (CHIP_SIZE, window_size), jnp.float32)
    for tap_index in range(TAP_COUNT):
        target = out_rows + shift_part[..., None, None] + (tap_index - TAP_COUNT // 2 + 1 + MARGIN)
        matrix = matrix + jnp.where(
            in_rows == target, weights[..., tap_index][..., None, None], 0.0
        )
    return matrix.astype(jnp.bfloat16)


def correlate(reference_tiles, resampled):
    chips_az = resampled.shape[-2] // CHIP_SIZE
    chips_rg = resampled.shape[-1] // CHIP_SIZE

    def as_chips(values):
        return values.astype(jnp.float32).reshape(
            values.shape[:-2] + (chips_az, CHIP_SIZE, chips_rg, CHIP_SIZE)
        )

    ref_chips = as_chips(reference_tiles)
    sec_chips = as_chips(resampled)
    ref_real = ref_chips[..., 0, :, :, :, :]
    ref_imag = ref_chips[..., 1, :, :, :, :]
    sec_real = sec_chips[..., 0, :, :, :, :]
    sec_imag = sec_chips[..., 1, :, :, :, :]
    cross_real = jnp.sum(ref_real * sec_real + ref_imag * sec_imag, axis=(-3, -1))
    cross_imag = jnp.sum(ref_imag * sec_real - ref_real * sec_imag, axis=(-3, -1))
    ref_power = jnp.sum(ref_real * ref_real + ref_imag * ref_imag, axis=(-3, -1))
    sec_power = jnp.sum(sec_real * sec_real + sec_imag * sec_imag, axis=(-3, -1))
    denominator = jnp.sqrt((ref_power + epsilon) * (sec_power + epsilon))
    return jnp.stack([cross_real / denominator, cross_imag / denominator])


def multilook_pairs(series):
    values = series.astype(jnp.float32)
    earlier = values[:-1]
    second = values[1:]
    early_real = earlier[:, :, 0]
    early_imag = earlier[:, :, 1]
    later_real = second[:, :, 0]
    later_imag = second[:, :, 1]
    cross_real = early_real * later_real + early_imag * later_imag
    cross_imag = early_imag * later_real - early_real * later_imag
    power_early = early_real * early_real + early_imag * early_imag
    power_later = later_real * later_real + later_imag * later_imag

    def box_sum(quantity):
        blocked = quantity.reshape(
            quantity.shape[:2]
            + (quantity.shape[2] // LOOK_AZ, LOOK_AZ, quantity.shape[3] // LOOK_RG, LOOK_RG)
        )
        return jnp.sum(blocked, axis=(3, 5))

    denominator = jnp.sqrt((box_sum(power_early) + epsilon) * (box_sum(power_later) + epsilon))
    return jnp.stack([box_sum(cross_real) / denominator, box_sum(cross_imag) / denominator])


def resample(padded, shift_part, fraction_part):
    window_size = CHIP_SIZE + 2 * MARGIN
    chips_az = shift_part.shape[3]
    chips_rg = shift_part.shape[4]
    pieces = [
        padded[
            :,
            :,
            :,
            chip_row * CHIP_SIZE : chip_row * CHIP_SIZE + window_size,
            chip_col * CHIP_SIZE : chip_col * CHIP_SIZE + window_size,
        ]
        for chip_row in range(chips_az)
        for chip_col in range(chips_rg)
    ]
    windows = jnp.stack(pieces, axis=3).reshape(
        padded.shape[:3] + (chips_az, chips_rg, window_size, window_size)
    )
    azimuth = sinc_matrix(shift_part[0], fraction_part[0])
    across = sinc_matrix(shift_part[1], fraction_part[1])
    partial_rows = jnp.einsum(
        "dtariw,dtcarwv->dtcariv", azimuth, windows, preferred_element_type=jnp.float32
    ).astype(jnp.bfloat16)
    chips_out = jnp.einsum(
        "dtcariv,dtarjv->dtcarij", partial_rows, across, preferred_element_type=jnp.float32
    ).astype(jnp.bfloat16)
    return chips_out.transpose(0, 1, 2, 3, 5, 4, 6).reshape(
        padded.shape[:3] + (chips_az * CHIP_SIZE, chips_rg * CHIP_SIZE)
    )


def per_device(acquisitions, shifts, fractions, ref_dates):
    dates_local = acquisitions.shape[0]
    tile_rows = acquisitions.shape[3] - 2 * MARGIN
    padded = padded_2(acquisitions, (("strip", 4),), MARGIN)
    owners = ref_dates // dates_local
    slots = ref_dates % dates_local
    candidates = [
        lax.dynamic_index_in_dim(acquisitions[:, tile_index], slots[tile_index], 0, keepdims=False)[
            :, MARGIN : MARGIN + tile_rows, :
        ]
        for tile_index in range(TILE_COUNT)
    ]
    reference_tiles = jnp.stack(
        [
            spread(candidates[tile_index], "date", owners[tile_index])
            for tile_index in range(TILE_COUNT)
        ]
    )
    resampled = resample(padded, shifts, fractions)
    chip_corr = correlate(reference_tiles, resampled)
    following = passed_along(resampled[0:1], "date", -1)
    series = jnp.concatenate([resampled, following], axis=0)
    looked = multilook_pairs(series)
    regrouped = lax.all_to_all(looked, "date", split_axis=3, concat_axis=1, tiled=True)
    coherence = regrouped[:, : dates_local * lax.axis_size("date") - 1]
    return (chip_corr, coherence)


def solution(mesh):
    return jax.shard_map(
        per_device,
        mesh=mesh,
        in_specs=(
            P("date", None, None, None, "strip"),
            P(None, "date", None, None, "strip"),
            P(None, "date", None, None, "strip"),
            P(),
        ),
        out_specs=(P(None, "date", None, None, "strip"), P(None, None, None, "date", "strip")),
        check_vma=False,
    )
```

profile of v0, /device:TPU:0, one launch (start us, length us, event | category | flops | bytes accessed | tf_op | source)
XLA Modules:
  0.0 226.9 jit_solution(10947532881645513688)
XLA Ops:
  9.5 4.9 %collective-permute-start = (bf16[2,2,2,344,12]{3,4,2,1,0:T(8,128)(2,1)S(1)}, bf16[2,2,2,344,12]{3,4,2,1,0:T(8,128)(2,1)S(1)}, u32[]{:S(2)}, u32[]{:S(2)}) collective-permute-start(bf16[2,2,2,344,12]{3,4,2,1,0:T(8,128)(2,1)S(1)} %get-tuple-element.29), channel_id=1, source_target_pairs={{0,1},{2,3},{4,5},{6,7},{8,9},{10,11},{12,13},{14,15},{16,17},{18,... | collective-permute-start | bytes 198152 | tf_op jit(solution)/shard_map/ppermute | solution.py:21
  26.9 3.2 %fusion.114 = (f32[2,2,5,5]{3,1,2,0:T(2,128)S(1)}, f32[2,2,5,5]{3,1,2,0:T(2,128)S(1)}) fusion(f32[2,2,5,5]{3,1,2,0:T(2,128)S(1)} %get-tuple-element.53, f32[8]{0:T(128)S(1)} %convert_add_fusion, f32[2,2,5,5]{3,1,2,0:T(2,128)S(1)} %get-tuple-element.52), kind=kLoop, calls=%fused_computation.187 | loop fusion | flops 62200 | bytes 1632 | tf_op jit(solution)/shard_map/reduce_sum | solution.py:46
  30.1 3.1 %broadcast_divide_fusion.1 = (f32[2,2,5,5,8]{3,1,2,0,4:T(2,128)S(1)}, f32[2,2,5,5,8]{3,1,2,0,4:T(2,128)S(1)}) fusion(f32[2,2,5,5]{3,1,2,0:T(2,128)S(1)} %get-tuple-element.16, f32[2,2,5,5]{3,1,2,0:T(2,128)S(1)} %get-tuple-element.53, f32[8]{0:T(128)S(1)} %convert_add_fusion, f32[2,2,5,5]{3,1,2,0:T(2,128)S(1)} %get-tuple-element.17, ...), kind=kLoop, calls=%fused_computation.185 | loop fusion | flops 62400 | bytes 8032 | tf_op jit(solution)/shard_map/div | solution.py:46
  58.0 7.2 %copy.165 = bf16[2,2,2,25,88,88]{5,4,2,3,1,0:T(8,128)(2,1)} copy(bf16[2,2,2,25,88,88]{4,5,2,1,0,3:T(8,128)(2,1)} %fusion.62) | data formatting | bytes 6195200 | tf_op jit(solution)/shard_map/stack | solution.py:120
  65.4 13.2 %fusion.4.clone.5 = bf16[2,2,2,5,5,64,88]{6,5,2,4,3,1,0:T(8,128)(2,1)S(1)} fusion(bf16[2,2,2,5,5,88,88]{6,5,2,4,3,1,0:T(8,128)(2,1)} %bitcast.221, f32[2,2,5,5]{3,2,1,0:T(8,128)S(1)} %copy.174, s32[2,2,5,5,64]{4,3,2,1,0:T(8,128)S(1)} %get-tuple-element.63, f32[2,2,5,5]{3,2,1,0:T(8,128)S(1)} %copy.173, ...), kind=kOutput, calls=%fused_computation.3.clone.clone.clone.clone.clone.2 | convolution fusion | flops 212889600 | bytes 5558400 | tf_op jit(solution)/shard_map/dtariw,dtcarwv->dtcariv/dot_general | solution.py:125
  78.7 13.6 %fusion.122 = (f32[2,2,2,5,64,5,64]{4,6,2,5,3,1,0:T(8,128)}, bf16[2,2,2,5,64,5,64]{4,6,2,5,3,1,0:T(8,128)(2,1)S(1)}) fusion(f32[2,2,5,5]{3,2,1,0:T(8,128)S(1)} %copy-done.13, s32[2,2,5,5,64]{4,3,2,1,0:T(8,128)S(1)} %copy-done.5, f32[2,2,5,5]{3,2,1,0:T(8,128)S(1)} %copy-done.12, s32[2,2,5,5,64]{4,3,2,1,0:T(8,128)S(1)} %copy-done.4, ...), kind=kOutput, calls=%fused_computation.226 | convolution fusion | flops 159334400 | bytes 7376000 | tf_op jit(solution)/shard_map/dtcariv,dtarjv->dtcarij/dot_general | solution.py:128
  93.7 5.2 %copy.181 = bf16[2,2,2,5,64,5,64]{6,5,4,3,2,1,0:T(8,128)(2,1)} copy(bf16[2,2,2,5,64,5,64]{4,6,2,5,3,1,0:T(8,128)(2,1)S(1)} %get-tuple-element.79) | data formatting | bytes 3276800 | tf_op jit(solution)/shard_map/convert_element_type | solution.py:130
  98.9 3.2 %copy.182 = bf16[1,2,2,5,64,5,64]{6,5,4,3,2,1,0:T(8,128)(2,1)S(1)} copy(bf16[1,2,2,5,64,5,64]{4,6,2,5,3,1,0:T(8,128)(2,1)} %slice.307) | data formatting | bytes 1638400 | tf_op jit(solution)/shard_map/slice | solution.py:156
  105.8 7.2 %reshape.241 = bf16[2,2,2,320,320]{4,3,2,1,0:T(8,128)(2,1)} reshape(bf16[2,2,2,5,64,5,64]{6,5,4,3,2,1,0:T(8,128)(2,1)} %copy.181) | data formatting | bytes 3276800 | tf_op jit(solution)/shard_map/reshape | solution.py:131
  113.0 19.2 %all-reduce.3.cloned.1.call-done = (bf16[1,2,5,64,5,64]{5,4,3,2,1,0:T(8,128)(2,1)}, bf16[1,2,5,64,5,64]{5,4,3,2,1,0:T(8,128)(2,1)}) async-done(((bf16[1,2,5,64,5,64]{5,4,3,2,1,0:T(8,128)(2,1)}, bf16[1,2,5,64,5,64]{5,4,3,2,1,0:T(8,128)(2,1)}), (bf16[1,2,5,64,5,64]{5,4,3,2,1,0:T(8,128)(2,1)}, bf16[1,2,5,64,5,64]{5,4,3,2,1,0:T(8,128)(2,1)})) %all-reduce.3.cloned.1.call-update) | async-done | bytes 819216 | tf_op jit(solution)/shard_map/psum | solution.py:31
  132.2 2.7 %maximum_convert_fusion.1 = f32[2,2,5,64,5,64]{5,4,3,2,1,0:T(8,128)S(1)} fusion(bf16[1,2,5,64,5,64]{5,4,3,2,1,0:T(8,128)(2,1)} %get-tuple-element.18, bf16[1,2,5,64,5,64]{5,4,3,2,1,0:T(8,128)(2,1)} %get-tuple-element.19), kind=kLoop, calls=%fused_computation.30 | loop fusion | flops 819200 | bytes 2457600 | tf_op jit(solution)/shard_map/convert_element_type | solution.py:63
  137.5 2.9 %copy.155 = f32[2,5,64,5,64]{2,4,3,1,0:T(8,128)} copy(f32[2,5,64,5,64]{4,3,2,1,0:T(8,128)} %get-tuple-element.24) | data formatting | bytes 1638400 | tf_op jit(solution)/shard_map/mul | solution.py:73
  142.0 5.0 %add_reduce_fusion.1 = (f32[2,2,5,5]{3,2,1,0:T(8,128)S(1)}, f32[2,2,5,5]{3,2,1,0:T(8,128)S(1)}, f32[2,2,5,5]{3,2,1,0:T(8,128)S(1)}) fusion(f32[2,2,2,5,64,5,64]{4,6,2,5,3,1,0:T(8,128)} %get-tuple-element.78, f32[2,5,64,5,64]{2,4,3,1,0:T(8,128)} %copy.176, f32[2,5,64,5,64]{2,4,3,1,0:T(8,128)} %copy.155), kind=kLoop, calls=%fused_computation.6 | loop fusion | flops 4914900 | bytes 4916400 | tf_op jit(solution)/shard_map/reduce_sum | solution.py:73
  148.9 2.8 %multiply_add_fusion.2 = (f32[2,2,1,320,320]{4,3,2,1,0:T(8,128)}, f32[2,2,1,320,320]{4,3,2,1,0:T(8,128)}, f32[2,2,1,320,320]{4,3,2,1,0:T(8,128)}, f32[2,2,1,320,320]{4,3,2,1,0:T(8,128)S(1)}) fusion(f32[3,2,2,320,320]{4,3,2,1,0:T(8,128)S(1)} %maximum_convert_fusion), kind=kLoop, calls=%fused_computation.35 | loop fusion | flops 4915200 | bytes 13107200 | tf_op jit(solution)/shard_map/add | solution.py:89
  151.7 9.1 %add.572 = f32[2,2,64,5,16,20]{5,4,3,2,1,0:T(8,128)} reshape(f32[2,2,1,320,320]{4,3,2,1,0:T(8,128)} %get-tuple-element.20) | data formatting | bytes 3276800 | tf_op jit(solution)/shard_map/add | solution.py:89
  160.8 9.0 %add.574 = f32[2,2,64,5,16,20]{5,4,3,2,1,0:T(8,128)} reshape(f32[2,2,1,320,320]{4,3,2,1,0:T(8,128)} %get-tuple-element.21) | data formatting | bytes 3276800 | tf_op jit(solution)/shard_map/add | solution.py:91
  169.8 4.8 %reduce_sum.102 = f32[2,2,64,16]{3,2,1,0:T(8,128)S(1)} reduce(f32[2,2,64,5,16,20]{5,4,3,2,1,0:T(8,128)} %add.572, f32[]{:T(128)} %constant.98.clone.1), dimensions={3,5}, to_apply=%region_8.10 | reduce | flops 405504 | bytes 1654788 | tf_op jit(solution)/shard_map/reduce_sum | solution.py:99
  174.6 4.8 %reduce_sum.103 = f32[2,2,64,16]{3,2,1,0:T(8,128)S(1)} reduce(f32[2,2,64,5,16,20]{5,4,3,2,1,0:T(8,128)} %add.574, f32[]{:T(128)} %constant.98.clone.1), dimensions={3,5}, to_apply=%region_9.11 | reduce | flops 405504 | bytes 1654788 | tf_op jit(solution)/shard_map/reduce_sum | solution.py:99
  179.4 9.1 %add.577 = f32[2,2,64,5,16,20]{5,4,3,2,1,0:T(8,128)} reshape(f32[2,2,1,320,320]{4,3,2,1,0:T(8,128)} %get-tuple-element.22) | data formatting | bytes 3276800 | tf_op jit(solution)/shard_map/add | solution.py:92
  188.5 4.8 %reduce_sum.104 = f32[2,2,64,16]{3,2,1,0:T(8,128)S(1)} reduce(f32[2,2,64,5,16,20]{5,4,3,2,1,0:T(8,128)} %add.577, f32[]{:T(128)} %constant.98.clone.1), dimensions={3,5}, to_apply=%region_10.12 | reduce | flops 405504 | bytes 1654788 | tf_op jit(solution)/shard_map/reduce_sum | solution.py:99
  193.3 7.9 %sub.65 = f32[2,2,64,5,16,20]{5,4,3,2,1,0:T(8,128)} reshape(f32[2,2,1,320,320]{4,3,2,1,0:T(8,128)S(1)} %get-tuple-element.23) | data formatting | bytes 3276800 | tf_op jit(solution)/shard_map/sub | solution.py:90
  201.2 4.8 %reduce_sum.105 = f32[2,2,64,16]{3,2,1,0:T(8,128)S(1)} reduce(f32[2,2,64,5,16,20]{5,4,3,2,1,0:T(8,128)} %sub.65, f32[]{:T(128)} %constant.98.clone.1), dimensions={3,5}, to_apply=%region_11.13 | reduce | flops 405504 | bytes 1654788 | tf_op jit(solution)/shard_map/reduce_sum | solution.py:99
  207.3 3.5 %all-to-all-start = ((f32[16,1,512]{2,1,0:T(1,128)}), f32[16,1,512]{2,1,0:T(1,128)S(1)}, u32[]{:S(2)}, u32[]{:S(2)}) async-start(f32[16,1,512]{2,1,0:T(1,128)} %reshape.244), calls=%async_computation | async-start | bytes 65536 | tf_op jit(solution)/shard_map/all_to_all | solution.py:159
  211.4 6.0 %all-to-all-done = f32[16,1,512]{2,1,0:T(1,128)S(1)} async-done(((f32[16,1,512]{2,1,0:T(1,128)}), f32[16,1,512]{2,1,0:T(1,128)S(1)}, u32[]{:S(2)}, u32[]{:S(2)}) %all-to-all-start) | async-done | bytes 32800 | tf_op jit(solution)/shard_map/all_to_all | solution.py:159
  (122 shorter events, 50.0 us)
Async XLA Ops:
  7.2 125.0 %all-reduce.3.cloned.1.call-start = ((), (), s32[]{:S(2)}) async-start(), calls=%async_computation.1 | async-start | bytes 5242880 | tf_op jit(solution)/shard_map/psum | solution.py:31
  8.2 33.4 %collective-permute-start.1 = (bf16[2,2,2,344,12]{3,4,2,1,0:T(8,128)(2,1)S(1)}, bf16[2,2,2,344,12]{3,4,2,1,0:T(8,128)(2,1)S(1)}, u32[]{:S(2)}, u32[]{:S(2)}) collective-permute-start(bf16[2,2,2,344,12]{3,4,2,1,0:T(8,128)(2,1)S(1)} %get-tuple-element.28), channel_id=1, source_target_pairs={{1,0},{3,2},{5,4},{7,6},{9,8},{11,10},{13,12},{15,14},{17,16},{19,... | collective-permute-start | bytes 198152 | tf_op jit(solution)/shard_map/ppermute | solution.py:24
  9.5 29.1 %collective-permute-start = (bf16[2,2,2,344,12]{3,4,2,1,0:T(8,128)(2,1)S(1)}, bf16[2,2,2,344,12]{3,4,2,1,0:T(8,128)(2,1)S(1)}, u32[]{:S(2)}, u32[]{:S(2)}) collective-permute-start(bf16[2,2,2,344,12]{3,4,2,1,0:T(8,128)(2,1)S(1)} %get-tuple-element.29), channel_id=1, source_target_pairs={{0,1},{2,3},{4,5},{6,7},{8,9},{10,11},{12,13},{14,15},{16,17},{18,... | collective-permute-start | bytes 198152 | tf_op jit(solution)/shard_map/ppermute | solution.py:21
  23.6 3.2 %copy-start.7 = (s32[2,2,2,5,5]{4,2,3,1,0:T(2,128)S(1)}, s32[2,2,2,5,5]{4,2,3,1,0:T(2,128)}, u32[]{:S(2)}) copy-start(s32[2,2,2,5,5]{4,2,3,1,0:T(2,128)} %param.6) | copy-start | bytes 2404
  23.6 3.3 %copy-start.8 = (s32[2,2,2,5,5]{4,2,3,1,0:T(2,128)S(1)}, s32[2,2,2,5,5]{4,2,3,1,0:T(2,128)}, u32[]{:S(2)}) copy-start(s32[2,2,2,5,5]{4,2,3,1,0:T(2,128)} %param.7) | copy-start | bytes 2404
  25.2 8.9 %copy-start = (bf16[2,2,2,344,320]{3,4,2,1,0:T(8,128)(2,1)S(1)}, bf16[2,2,2,344,320]{3,4,2,1,0:T(8,128)(2,1)}, u32[]{:S(2)}) copy-start(bf16[2,2,2,344,320]{3,4,2,1,0:T(8,128)(2,1)} %param.5) | copy-start | bytes 5283844
  58.0 7.3 %copy-start.15 = (f32[2,2,5,5]{3,2,1,0:T(8,128)S(1)}, f32[2,2,5,5]{3,2,1,0:T(8,128)}, u32[]{:S(2)}) copy-start(f32[2,2,5,5]{3,2,1,0:T(8,128)} %copy.168) | copy-start | bytes 1204
  65.3 13.3 %copy-start.2 = (s32[2,2,5,5,64]{4,3,2,1,0:T(8,128)S(1)}, s32[2,2,5,5,64]{4,3,2,1,0:T(8,128)}, u32[]{:S(2)}) copy-start(s32[2,2,5,5,64]{4,3,2,1,0:T(8,128)} %get-tuple-element.93) | copy-start | bytes 76804
  65.3 13.3 %copy-start.3 = (s32[2,2,5,5,64]{4,3,2,1,0:T(8,128)S(1)}, s32[2,2,5,5,64]{4,3,2,1,0:T(8,128)}, u32[]{:S(2)}) copy-start(s32[2,2,5,5,64]{4,3,2,1,0:T(8,128)} %get-tuple-element.94) | copy-start | bytes 76804
  65.3 13.3 %copy-start.4 = (s32[2,2,5,5,64]{4,3,2,1,0:T(8,128)S(1)}, s32[2,2,5,5,64]{4,3,2,1,0:T(8,128)}, u32[]{:S(2)}) copy-start(s32[2,2,5,5,64]{4,3,2,1,0:T(8,128)} %get-tuple-element.95) | copy-start | bytes 76804
  65.3 13.3 %copy-start.5 = (s32[2,2,5,5,64]{4,3,2,1,0:T(8,128)S(1)}, s32[2,2,5,5,64]{4,3,2,1,0:T(8,128)}, u32[]{:S(2)}) copy-start(s32[2,2,5,5,64]{4,3,2,1,0:T(8,128)} %get-tuple-element.96) | copy-start | bytes 76804
  65.3 13.3 %copy-start.6 = (s32[2,2,5,5,64]{4,3,2,1,0:T(8,128)S(1)}, s32[2,2,5,5,64]{4,3,2,1,0:T(8,128)}, u32[]{:S(2)}) copy-start(s32[2,2,5,5,64]{4,3,2,1,0:T(8,128)} %get-tuple-element.97) | copy-start | bytes 76804
  65.3 13.3 %copy-start.9 = (f32[2,2,5,5]{3,2,1,0:T(8,128)S(1)}, f32[2,2,5,5]{3,2,1,0:T(8,128)}, u32[]{:S(2)}) copy-start(f32[2,2,5,5]{3,2,1,0:T(8,128)} %copy.160) | copy-start | bytes 1204
  65.3 13.3 %copy-start.10 = (f32[2,2,5,5]{3,2,1,0:T(8,128)S(1)}, f32[2,2,5,5]{3,2,1,0:T(8,128)}, u32[]{:S(2)}) copy-start(f32[2,2,5,5]{3,2,1,0:T(8,128)} %copy.161) | copy-start | bytes 1204
  65.3 13.3 %copy-start.11 = (f32[2,2,5,5]{3,2,1,0:T(8,128)S(1)}, f32[2,2,5,5]{3,2,1,0:T(8,128)}, u32[]{:S(2)}) copy-start(f32[2,2,5,5]{3,2,1,0:T(8,128)} %copy.162) | copy-start | bytes 1204
  65.3 13.3 %copy-start.12 = (f32[2,2,5,5]{3,2,1,0:T(8,128)S(1)}, f32[2,2,5,5]{3,2,1,0:T(8,128)}, u32[]{:S(2)}) copy-start(f32[2,2,5,5]{3,2,1,0:T(8,128)} %copy.163) | copy-start | bytes 1204
  65.3 13.3 %copy-start.13 = (f32[2,2,5,5]{3,2,1,0:T(8,128)S(1)}, f32[2,2,5,5]{3,2,1,0:T(8,128)}, u32[]{:S(2)}) copy-start(f32[2,2,5,5]{3,2,1,0:T(8,128)} %copy.164) | copy-start | bytes 1204
  65.3 13.3 %copy-start.14 = (f32[2,2,5,5]{3,2,1,0:T(8,128)S(1)}, f32[2,2,5,5]{3,2,1,0:T(8,128)}, u32[]{:S(2)}) copy-start(f32[2,2,5,5]{3,2,1,0:T(8,128)} %copy.157) | copy-start | bytes 1204
  104.3 42.8 %collective-permute-start.2 = (bf16[1,2,2,320,320]{4,3,2,1,0:T(8,128)(2,1)}, bf16[1,2,2,320,320]{4,3,2,1,0:T(8,128)(2,1)}, u32[]{:S(2)}, u32[]{:S(2)}) collective-permute-start(bf16[1,2,2,320,320]{4,3,2,1,0:T(8,128)(2,1)} %slice.274), channel_id=1, source_target_pairs={{2,0},{4,2},{6,4},{8,6},{10,8},{12,10},{14,12},{16,14},{18,16},{20... | collective-permute-start | bytes 2457608 | tf_op jit(solution)/shard_map/ppermute | solution.py:37
  142.0 5.1 %copy-start.1 = (bf16[2,2,2,320,320]{4,3,2,1,0:T(8,128)(2,1)S(1)}, bf16[2,2,2,320,320]{4,3,2,1,0:T(8,128)(2,1)}, u32[]{:S(2)}) copy-start(bf16[2,2,2,320,320]{4,3,2,1,0:T(8,128)(2,1)} %reshape.241) | copy-start | bytes 4915204
  207.3 10.1 %all-to-all-start = ((f32[16,1,512]{2,1,0:T(1,128)}), f32[16,1,512]{2,1,0:T(1,128)S(1)}, u32[]{:S(2)}, u32[]{:S(2)}) async-start(f32[16,1,512]{2,1,0:T(1,128)} %reshape.244), calls=%async_computation | async-start | bytes 65536 | tf_op jit(solution)/shard_map/all_to_all | solution.py:159
Sparse Core Ops, SparseCore 0:
  26.9 105.2 all-reduce.2
where the time goes:
time: 228 us; the launch traced here: 227 us
  local copies, waits for them, and re-layouts  98.4 us (43%)
  other arithmetic  45.7 us (20%)
  matrix products  26.8 us (12%)
  waiting for transfers between devices  25.2 us (11%)
  between operations  19.6 us (9%)
  starting transfers between devices  11.2 us (5%)
    psum x1, waiting for transfers between devices, spread(): return lax.psum(kept, axis)  19.2 us
    reduce_sum x4, other arithmetic, box_sum(): return jnp.sum(blocked, axis=(3, 5))  19.2 us
    unnamed x55, local copies, waits for them, and re-layouts  17.1 us
    dot_general x1, matrix products, resample(): jnp.einsum('dtcariv,dtarjv->dtcarij', partial_rows, across, preferred_ele...  13.6 us
    dot_general x1, matrix products, resample(): jnp.einsum('dtariw,dtcarwv->dtcariv', azimuth, windows, preferred_element...  13.2 us
    add x1, local copies, waits for them, and re-layouts, multilook_pairs(): power_later = later_real * later_real + later_imag * later_imag  9.09 us
    add x1, local copies, waits for them, and re-layouts, multilook_pairs(): cross_real = early_real * later_real + early_imag * later_imag  9.08 us
    add x1, local copies, waits for them, and re-layouts, multilook_pairs(): power_early = early_real * early_real + early_imag * early_imag  9.02 us
  transfers between devices with their start and end apart: 5, of which 2 were waited for; matrix products, arithmetic and copies ran while one was open for 47% of the time, Pallas kernels for 0%

commit v1 on v0

--- a/solution.py
+++ b/solution.py
@@ -28,7 +28,8 @@
 
 def spread(value, axis, source):
     kept = jnp.where(lax.axis_index(axis) == source, value, 0).astype(value.dtype)
-    return lax.psum(kept, axis)
+    build_edge_now = lambda group_axis, z: jax.lax.all_gather(z, group_axis).sum(axis=0)
+    return build_edge_now(axis, kept)
 
 
 def passed_along(block, axis, distance):

time: 228 us -> 236 us (1.035)
  blocking collectives: 0 us -> 28.5 us
  waiting for transfers between devices: 25.2 us -> 0.06 us
  other arithmetic: 45.7 us -> 54.1 us
  starting transfers between devices: 11.2 us -> 7.72 us
    all_to_all x0 -> x1, blocking collectives: none -> 28.5 us  [per_device(): lax.all_to_all(looked, 'date', split_axis=3, concat_axis=1, tiled=True)]
    psum x1 -> x0, waiting for transfers between devices: 19.2 us -> none  [spread(): return lax.psum(kept, axis)]
    reduce_sum x0 -> x2, other arithmetic: none -> 9.32 us  [spread(): jax.lax.all_gather(z, group_axis).sum(axis=0)]
    all_to_all x1 -> x0, waiting for transfers between devices: 5.98 us -> none  [per_device(): lax.all_to_all(looked, 'date', split_axis=3, concat_axis=1, tiled=True)]
    broadcast_in_dim x17, local copies, waits for them, and re-layouts: 4.27 us -> 0.08 us  [sinc_matrix(): jnp.where(in_rows == target, weights[..., tap_index][..., None, None], 0.0)]
    dynamic_slice x0 -> x4, local copies, waits for them, and re-layouts: none -> 3.69 us  [per_device(): lax.dynamic_index_in_dim(acquisitions[:, tile_index], slots[tile_index],...]
    all_to_all x1 -> x0, starting transfers between devices: 3.5 us -> none  [per_device(): lax.all_to_all(looked, 'date', split_axis=3, concat_axis=1, tiled=True)]
    convert_element_type x1, local copies, waits for them, and re-layouts: 5.24 us -> 7.72 us  [resample(): chips_out = jnp.einsum('dtcariv,dtarjv->dtcarij', partial_rows, across, p...]
  transfers between devices with their start and end apart: 5 -> 5, of which waited for: 2 -> 0; matrix products, arithmetic and copies ran while one was open for 47% -> 63% of each run, Pallas kernels for 0% -> 0%
where the time goes in v1:
time: 236 us; the launch traced here: 235 us
  local copies, waits for them, and re-layouts  98 us (42%)
  other arithmetic  54.1 us (23%)
  blocking collectives  28.5 us (12%)
  matrix products  26.6 us (11%)
  between operations  19.8 us (8%)
  starting transfers between devices  7.72 us (3%)
    all_to_all x1, blocking collectives, per_device(): lax.all_to_all(looked, 'date', split_axis=3, concat_axis=1, tiled=True)  28.5 us
    reduce_sum x4, other arithmetic, box_sum(): return jnp.sum(blocked, axis=(3, 5))  19.8 us
    unnamed x31, local copies, waits for them, and re-layouts  18 us
    dot_general x1, matrix products, resample(): jnp.einsum('dtcariv,dtarjv->dtcarij', partial_rows, across, preferred_ele...  13.6 us
    dot_general x1, matrix products, resample(): jnp.einsum('dtariw,dtcarwv->dtcariv', azimuth, windows, preferred_element...  13 us
    reduce_sum x2, other arithmetic, spread(): jax.lax.all_gather(z, group_axis).sum(axis=0)  9.32 us
    add x1, local copies, waits for them, and re-layouts, multilook_pairs(): power_later = later_real * later_real + later_imag * later_imag  9.12 us
    add x1, local copies, waits for them, and re-layouts, multilook_pairs(): cross_real = early_real * later_real + early_imag * later_imag  9.12 us
  transfers between devices with their start and end apart: 5, of which 0 were waited for; matrix products, arithmetic and copies ran while one was open for 63% of the time, Pallas kernels for 0%

profile of v1, /device:TPU:0, one launch (start us, length us, event | category | flops | bytes accessed | tf_op | source)
XLA Modules:
  0.0 234.8 jit_solution(14353365737267427088)
XLA Ops:
  23.5 4.9 %collective-permute-start = (bf16[2,2,2,344,12]{3,4,2,1,0:T(8,128)(2,1)S(1)}, bf16[2,2,2,344,12]{3,4,2,1,0:T(8,128)(2,1)S(1)}, u32[]{:S(2)}, u32[]{:S(2)}) collective-permute-start(bf16[2,2,2,344,12]{3,4,2,1,0:T(8,128)(2,1)S(1)} %get-tuple-element.25), channel_id=1, source_target_pairs={{0,1},{2,3},{4,5},{6,7},{8,9},{10,11},{12,13},{14,15},{16,17},{18,... | collective-permute-start | bytes 198152 | tf_op jit(solution)/shard_map/ppermute | solution.py:21
  28.5 3.2 %fusion.114 = (f32[2,2,5,5]{3,1,2,0:T(2,128)S(1)}, f32[2,2,5,5]{3,1,2,0:T(2,128)S(1)}) fusion(f32[2,2,5,5]{3,1,2,0:T(2,128)S(1)} %get-tuple-element.49, f32[8]{0:T(128)S(1)} %convert_add_fusion, f32[2,2,5,5]{3,1,2,0:T(2,128)S(1)} %get-tuple-element.48), kind=kLoop, calls=%fused_computation.185 | loop fusion | flops 62200 | bytes 1632 | tf_op jit(solution)/shard_map/reduce_sum | solution.py:47
  31.7 3.1 %broadcast_divide_fusion.1 = (f32[2,2,5,5,8]{3,1,2,0,4:T(2,128)S(1)}, f32[2,2,5,5,8]{3,1,2,0,4:T(2,128)S(1)}) fusion(f32[2,2,5,5]{3,1,2,0:T(2,128)S(1)} %get-tuple-element.14, f32[2,2,5,5]{3,1,2,0:T(2,128)S(1)} %get-tuple-element.49, f32[8]{0:T(128)S(1)} %convert_add_fusion, f32[2,2,5,5]{3,1,2,0:T(2,128)S(1)} %get-tuple-element.15, ...), kind=kLoop, calls=%fused_computation.183 | loop fusion | flops 62400 | bytes 8032 | tf_op jit(solution)/shard_map/div | solution.py:47
  54.7 7.2 %copy.148 = bf16[2,2,2,25,88,88]{5,4,2,3,1,0:T(8,128)(2,1)} copy(bf16[2,2,2,25,88,88]{4,5,2,1,0,3:T(8,128)(2,1)} %fusion.62) | data formatting | bytes 6195200 | tf_op jit(solution)/shard_map/stack | solution.py:121
  61.9 13.0 %fusion.4.clone.5 = bf16[2,2,2,5,5,64,88]{6,5,2,4,3,1,0:T(8,128)(2,1)S(1)} fusion(bf16[2,2,2,5,5,88,88]{6,5,2,4,3,1,0:T(8,128)(2,1)} %bitcast.223, f32[2,2,5,5]{3,2,1,0:T(8,128)S(1)} %copy.157, s32[2,2,5,5,64]{4,3,2,1,0:T(8,128)S(1)} %get-tuple-element.59, f32[2,2,5,5]{3,2,1,0:T(8,128)S(1)} %copy.156, ...), kind=kOutput, calls=%fused_computation.3.clone.clone.clone.clone.clone.2 | convolution fusion | flops 212889600 | bytes 5558400 | tf_op jit(solution)/shard_map/dtariw,dtcarwv->dtcariv/dot_general | solution.py:126
  75.0 13.6 %fusion.122 = (f32[2,2,2,5,64,5,64]{4,6,2,5,3,1,0:T(8,128)}, bf16[2,2,2,5,64,5,64]{4,6,2,5,3,1,0:T(8,128)(2,1)S(1)}) fusion(f32[2,2,5,5]{3,2,1,0:T(8,128)S(1)} %copy.147, s32[2,2,5,5,64]{4,3,2,1,0:T(8,128)S(1)} %get-tuple-element.92, f32[2,2,5,5]{3,2,1,0:T(8,128)S(1)} %copy.146, s32[2,2,5,5,64]{4,3,2,1,0:T(8,128)S(1)} %get-tuple-element.91, ...), kind=kOutput, calls=%fused_computation.226 | convolution fusion | flops 159334400 | bytes 7376000 | tf_op jit(solution)/shard_map/dtcariv,dtarjv->dtcarij/dot_general | solution.py:129
  90.4 2.8 %copy.165 = bf16[1,2,2,5,64,5,64]{6,5,4,3,2,1,0:T(8,128)(2,1)} copy(bf16[1,2,2,5,64,5,64]{4,6,2,5,3,1,0:T(8,128)(2,1)S(1)} %slice.307) | data formatting | bytes 1638400 | tf_op jit(solution)/shard_map/slice | solution.py:157
  93.2 3.3 %slice.274 = bf16[1,2,2,320,320]{4,3,2,1,0:T(8,128)(2,1)S(1)} reshape(bf16[1,2,2,5,64,5,64]{6,5,4,3,2,1,0:T(8,128)(2,1)} %copy.165) | data formatting | bytes 1638400 | tf_op jit(solution)/shard_map/slice | solution.py:157
  98.0 7.7 %copy.164 = bf16[2,2,2,5,64,5,64]{6,5,4,3,2,1,0:T(8,128)(2,1)} copy(bf16[2,2,2,5,64,5,64]{4,6,2,5,3,1,0:T(8,128)(2,1)} %copy-done.1) | data formatting | bytes 3276800 | tf_op jit(solution)/shard_map/convert_element_type | solution.py:131
  105.7 6.1 %reshape.241 = bf16[2,2,2,320,320]{4,3,2,1,0:T(8,128)(2,1)S(1)} reshape(bf16[2,2,2,5,64,5,64]{6,5,4,3,2,1,0:T(8,128)(2,1)} %copy.164) | data formatting | bytes 3276800 | tf_op jit(solution)/shard_map/reshape | solution.py:132
  113.6 2.9 %multiply_add_fusion.2 = (f32[2,2,1,320,320]{4,3,2,1,0:T(8,128)}, f32[2,2,1,320,320]{4,3,2,1,0:T(8,128)}, f32[2,2,1,320,320]{4,3,2,1,0:T(8,128)}, f32[2,2,1,320,320]{4,3,2,1,0:T(8,128)S(1)}) fusion(f32[3,2,2,320,320]{4,3,2,1,0:T(8,128)S(1)} %maximum_convert_fusion), kind=kLoop, calls=%fused_computation.35 | loop fusion | flops 4915200 | bytes 13107200 | tf_op jit(solution)/shard_map/add | solution.py:90
  116.4 9.1 %add.568 = f32[2,2,64,5,16,20]{5,4,3,2,1,0:T(8,128)} reshape(f32[2,2,1,320,320]{4,3,2,1,0:T(8,128)} %get-tuple-element.16) | data formatting | bytes 3276800 | tf_op jit(solution)/shard_map/add | solution.py:90
  125.5 9.0 %add.570 = f32[2,2,64,5,16,20]{5,4,3,2,1,0:T(8,128)} reshape(f32[2,2,1,320,320]{4,3,2,1,0:T(8,128)} %get-tuple-element.17) | data formatting | bytes 3276800 | tf_op jit(solution)/shard_map/add | solution.py:92
  134.6 4.8 %reduce_sum.128 = f32[2,2,64,16]{3,2,1,0:T(8,128)S(1)} reduce(f32[2,2,64,5,16,20]{5,4,3,2,1,0:T(8,128)} %add.568, f32[]{:T(128)} %constant.100.clone.1), dimensions={3,5}, to_apply=%region_8.10 | reduce | flops 405504 | bytes 1654788 | tf_op jit(solution)/shard_map/reduce_sum | solution.py:100
  139.4 4.9 %reduce_sum.129 = f32[2,2,64,16]{3,2,1,0:T(8,128)S(1)} reduce(f32[2,2,64,5,16,20]{5,4,3,2,1,0:T(8,128)} %add.570, f32[]{:T(128)} %constant.100.clone.1), dimensions={3,5}, to_apply=%region_9.11 | reduce | flops 405504 | bytes 1654788 | tf_op jit(solution)/shard_map/reduce_sum | solution.py:100
  144.3 9.1 %add.573 = f32[2,2,64,5,16,20]{5,4,3,2,1,0:T(8,128)} reshape(f32[2,2,1,320,320]{4,3,2,1,0:T(8,128)} %get-tuple-element.18) | data formatting | bytes 3276800 | tf_op jit(solution)/shard_map/add | solution.py:93
  153.4 5.0 %reduce_sum.130 = f32[2,2,64,16]{3,2,1,0:T(8,128)S(1)} reduce(f32[2,2,64,5,16,20]{5,4,3,2,1,0:T(8,128)} %add.573, f32[]{:T(128)} %constant.100.clone.1), dimensions={3,5}, to_apply=%region_10.12 | reduce | flops 405504 | bytes 1654788 | tf_op jit(solution)/shard_map/reduce_sum | solution.py:100
  158.4 8.0 %sub.65 = f32[2,2,64,5,16,20]{5,4,3,2,1,0:T(8,128)} reshape(f32[2,2,1,320,320]{4,3,2,1,0:T(8,128)S(1)} %get-tuple-element.19) | data formatting | bytes 3276800 | tf_op jit(solution)/shard_map/sub | solution.py:91
  166.4 5.0 %reduce_sum.131 = f32[2,2,64,16]{3,2,1,0:T(8,128)S(1)} reduce(f32[2,2,64,5,16,20]{5,4,3,2,1,0:T(8,128)} %sub.65, f32[]{:T(128)} %constant.100.clone.1), dimensions={3,5}, to_apply=%region_11.13 | reduce | flops 405504 | bytes 1654788 | tf_op jit(solution)/shard_map/reduce_sum | solution.py:100
  172.1 28.5 %all_to_all.18 = f32[16,1,512]{2,1,0:T(1,128)S(1)} all-to-all(f32[16,1,512]{2,1,0:T(1,128)S(1)} %reshape.246), channel_id=1, replica_groups=mesh['date'=16,'strip'=2] {'date'}, dimensions={0} | all-to-all | bytes 65536 | tf_op jit(solution)/shard_map/all_to_all | solution.py:160
  203.3 4.7 %reduce_sum.118 = bf16[2,320,320]{2,1,0:T(8,128)(2,1)S(1)} reduce(bf16[16,2,320,320]{3,2,1,0:T(8,128)(2,1)} %bitcast.221, bf16[]{:T(256)} %constant.94.clone.1), dimensions={0}, to_apply=%region_0.1 | reduce | flops 3072000 | bytes 6963202 | tf_op jit(solution)/shard_map/reduce_sum | solution.py:31
  208.0 4.7 %reduce_sum.119 = bf16[2,320,320]{2,1,0:T(8,128)(2,1)S(1)} reduce(bf16[16,2,320,320]{3,2,1,0:T(8,128)(2,1)} %bitcast.222, bf16[]{:T(256)} %constant.94.clone.1), dimensions={0}, to_apply=%region_1.2 | reduce | flops 3072000 | bytes 6963202 | tf_op jit(solution)/shard_map/reduce_sum | solution.py:31
  220.0 2.9 %copy.159 = f32[2,5,64,5,64]{2,4,3,1,0:T(8,128)} copy(f32[2,5,64,5,64]{4,3,2,1,0:T(8,128)} %get-tuple-element.21) | data formatting | bytes 1638400 | tf_op jit(solution)/shard_map/mul | solution.py:74
  222.9 4.4 %add_reduce_fusion.1 = (f32[2,2,5,5]{3,2,1,0:T(8,128)S(1)}, f32[2,2,5,5]{3,2,1,0:T(8,128)S(1)}, f32[2,2,5,5]{3,2,1,0:T(8,128)S(1)}) fusion(f32[2,2,2,5,64,5,64]{4,6,2,5,3,1,0:T(8,128)} %get-tuple-element.74, f32[2,5,64,5,64]{2,4,3,1,0:T(8,128)} %copy.159, f32[2,5,64,5,64]{2,4,3,1,0:T(8,128)S(1)} %copy.138), kind=kLoop, calls=%fused_computation.6 | loop fusion | flops 4914900 | bytes 4916400 | tf_op jit(solution)/shard_map/reduce_sum | solution.py:74
  (102 shorter events, 47.2 us)
Async XLA Ops:
  7.2 196.1 %all-gather.5.cloned.1.call-start = ((), (), s32[]{:S(2)}) async-start(), calls=%async_computation.1 | async-start | bytes 8355840 | tf_op jit(solution)/shard_map/all_gather | solution.py:31
  13.2 8.9 %copy-start = (bf16[2,2,2,344,320]{3,4,2,1,0:T(8,128)(2,1)S(1)}, bf16[2,2,2,344,320]{3,4,2,1,0:T(8,128)(2,1)}, u32[]{:S(2)}) copy-start(bf16[2,2,2,344,320]{3,4,2,1,0:T(8,128)(2,1)} %param.5) | copy-start | bytes 5283844
  15.3 13.2 %copy-start.2 = (s32[2,2,2,5,5]{4,2,3,1,0:T(2,128)S(1)}, s32[2,2,2,5,5]{4,2,3,1,0:T(2,128)}, u32[]{:S(2)}) copy-start(s32[2,2,2,5,5]{4,2,3,1,0:T(2,128)} %param.6) | copy-start | bytes 2404
  15.3 13.2 %copy-start.3 = (s32[2,2,2,5,5]{4,2,3,1,0:T(2,128)S(1)}, s32[2,2,2,5,5]{4,2,3,1,0:T(2,128)}, u32[]{:S(2)}) copy-start(s32[2,2,2,5,5]{4,2,3,1,0:T(2,128)} %param.7) | copy-start | bytes 2404
  18.2 189.7 %all-gather.7.cloned.1.call-start = ((), (), s32[]{:S(2)}) async-start(), calls=%async_computation.2 | async-start | bytes 8355840 | tf_op jit(solution)/shard_map/all_gather | solution.py:31
  22.2 13.3 %collective-permute-start.1 = (bf16[2,2,2,344,12]{3,4,2,1,0:T(8,128)(2,1)S(1)}, bf16[2,2,2,344,12]{3,4,2,1,0:T(8,128)(2,1)S(1)}, u32[]{:S(2)}, u32[]{:S(2)}) collective-permute-start(bf16[2,2,2,344,12]{3,4,2,1,0:T(8,128)(2,1)S(1)} %get-tuple-element.24), channel_id=1, source_target_pairs={{1,0},{3,2},{5,4},{7,6},{9,8},{11,10},{13,12},{15,14},{17,16},{19,... | collective-permute-start | bytes 198152 | tf_op jit(solution)/shard_map/ppermute | solution.py:24
  23.5 12.1 %collective-permute-start = (bf16[2,2,2,344,12]{3,4,2,1,0:T(8,128)(2,1)S(1)}, bf16[2,2,2,344,12]{3,4,2,1,0:T(8,128)(2,1)S(1)}, u32[]{:S(2)}, u32[]{:S(2)}) collective-permute-start(bf16[2,2,2,344,12]{3,4,2,1,0:T(8,128)(2,1)S(1)} %get-tuple-element.25), channel_id=1, source_target_pairs={{0,1},{2,3},{4,5},{6,7},{8,9},{10,11},{12,13},{14,15},{16,17},{18,... | collective-permute-start | bytes 198152 | tf_op jit(solution)/shard_map/ppermute | solution.py:21
  88.5 1.7 copy-start.1
  96.5 15.3 %collective-permute-start.2 = (bf16[1,2,2,320,320]{4,3,2,1,0:T(8,128)(2,1)S(1)}, bf16[1,2,2,320,320]{4,3,2,1,0:T(8,128)(2,1)}, u32[]{:S(2)}, u32[]{:S(2)}) collective-permute-start(bf16[1,2,2,320,320]{4,3,2,1,0:T(8,128)(2,1)S(1)} %slice.274), channel_id=1, source_target_pairs={{2,0},{4,2},{6,4},{8,6},{10,8},{12,10},{14,12},{16,14},{18,16},{20... | collective-permute-start | bytes 2457608 | tf_op jit(solution)/shard_map/ppermute | solution.py:38
Sparse Core Ops, SparseCore 0:
  18.4 73.6 all-gather.4
  94.4 76.3 all-gather.6
